TPU v7x, 256 devices: a whole 4x4x8 slice. The times are simulated.
256 devices in a mesh: seq: 32 (over y_lo, z, core), tp: 4 (over x), dp: 2 (over y_hi).
Axes of the slice: x: 4, y: 4 (y_hi: 2, y_lo: 2; y = y_hi * 2 + y_lo), z: 8, core: 2. Of those that a mesh axis runs over, the one named last changes fastest.
Arguments:
- query_gate: bfloat16 [2, 8192, 4096], P('dp', 'seq', 'tp'), may hold values from -6 to 6
- key_gate: bfloat16 [2, 8192, 4096], P('dp', 'seq', 'tp'), may hold values from -6 to 6
- value_input: bfloat16 [2, 8192, 4096], P('dp', 'seq', 'tp'), may hold values from -6 to 6
- filter_taps: bfloat16 [4096, 128], P('tp'), may hold values from -0.5 to 0.5
- skip_gain: float32 [4096], P('tp'), may hold values from -1 to 1
- out_weight: bfloat16 [4096, 4096], P('tp', 'dp'), may hold values from -0.09375 to 0.09375
- cotangent: bfloat16 [2, 8192, 4096], P('dp', 'seq', 'tp'), may hold values from -6 to 6
Outputs:
- grad_query: bfloat16 [2, 8192, 4096], P('dp', 'seq', 'tp')
- grad_key: bfloat16 [2, 8192, 4096], P('dp', 'seq', 'tp')
- grad_value: bfloat16 [2, 8192, 4096], P('dp', 'seq', 'tp')
- grad_filter: float32 [4096, 128], P('tp')
- grad_skip: float32 [4096], P('tp')
- grad_weight: float32 [4096, 4096], P(('seq', 'dp'), 'tp')
All inputs are finite; a program needn't handle non-finite values.
Results may differ from a plain program's by a relative error of at most 0.0095.
Values may be sent and summed in bfloat16 or wider, within the bound.
A program may use at most 192 MiB of HBM per device.

v0:
```python
import math
import jax
import jax.numpy as jnp
from jax import lax
from jax.sharding import PartitionSpec as P

block_rows = 16


def shifted(block, axis, distance):
    devices = range(lax.axis_size(axis))
    route = [(i - distance, i) for i in devices if i - distance in devices]
    return lax.ppermute(block, axis, route)


def taps_matrix(vector, row_count, col_count):
    channels, width_all = vector.shape
    tiled = jnp.tile(vector, (1, row_count + 1))
    skewed = tiled[:, : row_count * (width_all - 1)].reshape(channels, row_count, width_all - 1)
    return skewed[:, :, row_count - 1 : row_count - 1 + col_count]


def forward_table(filter_taps):
    channels, tap_count = filter_taps.shape
    padding = jnp.zeros((channels, block_rows), filter_taps.dtype)
    vector = jnp.concatenate([padding, filter_taps[:, ::-1], padding], axis=1)
    return taps_matrix(vector, block_rows, tap_count + block_rows)


def backward_table(filter_taps):
    channels, tap_count = filter_taps.shape
    before = jnp.zeros((channels, block_rows - 1), filter_taps.dtype)
    after = jnp.zeros((channels, block_rows + 1), filter_taps.dtype)
    vector = jnp.concatenate([before, filter_taps, after], axis=1)
    return taps_matrix(vector, block_rows, tap_count + block_rows)


def windows(extended, length, tap_count):
    pieces = []
    for shift_index in range(tap_count // block_rows + 1):
        lower = shift_index * block_rows
        pieces.append(
            extended[lower : lower + length].reshape(
                length // block_rows, block_rows, extended.shape[1]
            )
        )
    return jnp.concatenate(pieces, axis=1)


def lag_sums(blocks, tap_count):
    channels, row_count, col_count = blocks.shape
    flattened = blocks.reshape(channels, row_count * col_count)
    padded = jnp.concatenate([flattened, jnp.zeros((channels, row_count), blocks.dtype)], axis=1)
    diagonal = padded.reshape(channels, row_count, col_count + 1)[:, :, 1 : tap_count + 1]
    return jnp.sum(diagonal, axis=1)[:, ::-1]


def per_device(query_gate, key_gate, value_input, filter_taps, skip_gain, out_weight, cotangent):
    queries = query_gate[0]
    key_rows = key_gate[0]
    value_rows = value_input[0]
    length, channels = queries.shape
    tap_count = filter_taps.shape[1]
    seq_count = lax.axis_size("seq")
    replica_count = lax.axis_size("dp")
    norm_factor = 1.0 / math.sqrt(length * seq_count * replica_count)
    mixed = (key_rows.astype(jnp.float32) * value_rows.astype(jnp.float32)).astype(jnp.bfloat16)
    tail_rows = mixed[length - (tap_count - 1) :]
    prior = shifted(tail_rows, "seq", 1)
    extended = jnp.concatenate([jnp.zeros((1, channels), jnp.bfloat16), prior, mixed], axis=0)
    forward_windows = windows(extended, length, tap_count)
    conv = jnp.einsum(
        "cab,ibc->iac",
        forward_table(filter_taps),
        forward_windows,
        preferred_element_type=jnp.float32,
    ).reshape(length, channels)
    state = conv + skip_gain[None, :] * mixed.astype(jnp.float32)
    gated = (queries.astype(jnp.float32) * state).astype(jnp.bfloat16)
    full_cot = lax.all_gather(cotangent[0], "tp", axis=1, tiled=True)
    selected = full_cot
    grad_gated = lax.dot_general(
        selected,
        lax.all_gather(out_weight, "dp", axis=1, tiled=True),
        (((1,), (1,)), ((), ())),
        preferred_element_type=jnp.float32,
    )
    grad_query = (grad_gated * state).astype(jnp.bfloat16)
    signal = (grad_gated * queries.astype(jnp.float32)).astype(jnp.bfloat16)
    head_rows = signal[: tap_count - 1]
    later = shifted(head_rows, "seq", -1)
    signal_ext = jnp.concatenate([signal, later, jnp.zeros((1, channels), jnp.bfloat16)], axis=0)
    back = jnp.einsum(
        "cab,ibc->iac",
        backward_table(filter_taps),
        windows(signal_ext, length, tap_count),
        preferred_element_type=jnp.float32,
    ).reshape(length, channels)
    back = back + skip_gain[None, :] * signal.astype(jnp.float32)
    grad_key = (back * value_rows.astype(jnp.float32)).astype(jnp.bfloat16)
    grad_value = (back * key_rows.astype(jnp.float32)).astype(jnp.bfloat16)
    signal_blocks = signal.reshape(length // block_rows, block_rows, channels)
    blocks = jnp.einsum(
        "iac,ibc->cab", signal_blocks, forward_windows, preferred_element_type=jnp.float32
    )
    skip_term = jnp.sum(signal.astype(jnp.float32) * mixed.astype(jnp.float32), axis=0)
    filter_sum, skip_sum = lax.psum((lag_sums(blocks, tap_count), skip_term), ("seq", "dp"))
    selected = full_cot
    grad_weight = lax.psum_scatter(
        lax.dot_general(
            selected, gated, (((0,), (0,)), ((), ())), preferred_element_type=jnp.float32
        ),
        ("seq", "dp"),
        scatter_dimension=0,
        tiled=True,
    )
    return (
        grad_query[None],
        grad_key[None],
        grad_value[None],
        filter_sum * norm_factor,
        skip_sum * norm_factor,
        grad_weight * norm_factor,
    )


def solution(mesh):
    return jax.shard_map(
        per_device,
        mesh=mesh,
        in_specs=(
            P("dp", "seq", "tp"),
            P("dp", "seq", "tp"),
            P("dp", "seq", "tp"),
            P("tp", None),
            P("tp"),
            P("tp", "dp"),
            P("dp", "seq", "tp"),
        ),
        out_specs=(
            P("dp", "seq", "tp"),
            P("dp", "seq", "tp"),
            P("dp", "seq", "tp"),
            P("tp", None),
            P("tp"),
            P(("seq", "dp"), "tp"),
        ),
        check_vma=False,
    )
```

profile of v0, /device:TPU:64, one launch (start us, length us, event | category | flops | bytes accessed | tf_op | source)
XLA Modules:
  0.0 1021.4 jit_solution(6205468329109296625)
XLA Ops:
  7.2 0.7 all-gather.6.cloned.1.call-update
  7.9 0.7 all-gather.4.cloned.1.call-update
  8.8 3.5 rev.6
  12.3 1.2 maximum_maximum_fusion
  13.7 0.7 tile.20
  14.4 2.9 slice.134
  17.3 4.8 reshape.123
  22.1 7.0 slice.135
  29.0 12.7 %copy.93 = bf16[1024,16,144]{2,1,0:T(8,128)(2,1)} copy(bf16[1024,16,144]{0,2,1:T(8,128)(2,1)} %slice.135) | data formatting | bytes 9437184
  41.8 3.7 all-gather.6.cloned.1.call-done
  45.5 112.5 %all-gather.4.cloned.1.call-done = bf16[1024,4096]{1,0:T(8,128)(2,1)} async-done(((bf16[1024,2048]{1,0:T(8,128)(2,1)}), bf16[1024,4096]{1,0:T(8,128)(2,1)}) %all-gather.4.cloned.1.call-update) | async-done | bytes 8388624 | tf_op jit(solution)/shard_map/all_gather | solution.py:84
  158.0 7.5 fusion.8
  165.5 0.7 slice.121
  166.2 2.4 collective-permute-start.1
  168.9 4.7 copy.70
  174.1 0.7 tile.8
  174.8 2.9 slice.119
  177.7 4.9 reshape.112
  182.6 6.8 slice.120
  189.4 12.5 %copy.92 = bf16[1024,16,144]{2,1,0:T(8,128)(2,1)} copy(bf16[1024,16,144]{0,2,1:T(8,128)(2,1)} %slice.120) | data formatting | bytes 9437184
  201.9 4.8 copy.74
  206.7 0.8 slice.106
  207.5 2.6 collective-permute-start
  210.1 2.8 pad_maximum_fusion
  212.9 5.8 copy.75
  218.7 5.8 copy.76
  224.4 5.7 copy.77
  230.1 5.7 copy.78
  235.8 4.8 copy.79
  240.6 4.7 copy.80
  245.2 4.7 copy.81
  249.9 4.7 copy.82
  254.6 35.9 %concatenate.45 = bf16[16,144,1024]{1,0,2:T(8,128)(2,1)} concatenate(bf16[16,16,1024]{1,0,2:T(8,128)(2,1)} %copy.74, bf16[16,16,1024]{1,0,2:T(8,128)(2,1)} %copy.75, bf16[16,16,1024]{1,0,2:T(8,128)(2,1)} %copy.76, bf16[16,16,1024]{1,0,2:T(8,128)(2,1)} %copy.77, bf16[16,16,1024]{1,0,2:T(8,128)(2,1)} %copy.78, bf16[16,16,1024]{1,0,2:T(8,128)(2,1)} %copy.79, ...), dimensions={1} | concatenate | bytes 9437184 | tf_op jit(solution)/shard_map/concatenate | solution.py:47
  290.6 11.3 %convolution_bitcast_fusion.1 = f32[16,16,1024]{1,0,2:T(8,128)} fusion(bf16[16,144,1024]{1,0,2:T(8,128)(2,1)} %concatenate.45, bf16[1024,16,144]{2,1,0:T(8,128)(2,1)} %copy.93), kind=kOutput, calls=%fused_computation.2 | convolution fusion | flops 75497472 | bytes 10485760 | tf_op jit(solution)/shard_map/cab,ibc->iac/dot_general | solution.py:93
  301.8 5.1 copy.85
  307.0 1.9 pad_maximum_fusion.3
  308.9 5.7 copy.62
  314.6 5.7 copy.63
  320.3 5.8 copy.64
  326.1 5.7 copy.65
  331.8 5.9 copy.66
  337.7 5.7 copy.67
  343.3 4.8 copy.68
  348.1 4.7 copy.69
  352.8 35.9 %concatenate.41 = bf16[16,144,1024]{1,0,2:T(8,128)(2,1)} concatenate(bf16[16,16,1024]{1,0,2:T(8,128)(2,1)} %copy.62, bf16[16,16,1024]{1,0,2:T(8,128)(2,1)} %copy.63, bf16[16,16,1024]{1,0,2:T(8,128)(2,1)} %copy.64, bf16[16,16,1024]{1,0,2:T(8,128)(2,1)} %copy.65, bf16[16,16,1024]{1,0,2:T(8,128)(2,1)} %copy.66, bf16[16,16,1024]{1,0,2:T(8,128)(2,1)} %copy.67, ...), dimensions={1} | concatenate | bytes 9437184 | tf_op jit(solution)/shard_map/concatenate | solution.py:47
  388.7 9.9 fusion.29
  398.6 11.3 %convolution_bitcast_fusion.2 = f32[16,16,1024]{1,0,2:T(8,128)} fusion(bf16[16,144,1024]{1,0,2:T(8,128)(2,1)} %concatenate.41, bf16[1024,16,144]{2,1,0:T(8,128)(2,1)} %copy.92), kind=kOutput, calls=%fused_computation.3 | convolution fusion | flops 75497472 | bytes 10485760 | tf_op jit(solution)/shard_map/cab,ibc->iac/dot_general | solution.py:72
  409.9 5.1 copy.73
  415.0 15.0 %copy.87 = f32[1024,16,144]{0,2,1:T(8,128)} copy(f32[1024,16,144]{2,1,0:T(8,128)} %fusion.29) | data formatting | bytes 18874368 | tf_op jit(solution)/shard_map/iac,ibc->cab/dot_general | solution.py:103
  430.0 9.3 concatenate.47
  439.3 10.3 %reshape.126 = f32[1024,16,145]{0,2,1:T(8,128)} reshape(f32[1024,2320]{0,1:T(8,128)} %concatenate.47) | data formatting | bytes 19005440 | tf_op jit(solution)/shard_map/reshape | solution.py:54
  449.6 5.5 slice_reduce_fusion
  455.1 4.7 rev.7
  460.2 3.5 fusion.14
  463.7 8.1 convolution_bitcast_fusion
  471.8 17.5 %copy.90 = f32[4096,1024]{1,0:T(8,128)} copy(f32[4096,1024]{0,1:T(8,128)} %convolution_bitcast_fusion) | data formatting | bytes 33554432
  489.4 124.9 %psum.15 = f32[1024]{0:T(1024)S(1)} all-reduce(f32[1024]{0:T(1024)S(1)} %get-tuple-element.24), channel_id=1, replica_groups=mesh['seq'=32,'tp'=4,'dp'=2] {'seq','dp'}, use_global_device_ids=true, to_apply=%region_3.0 | all-reduce | flops 1024 | bytes 8192 | tf_op jit(solution)/shard_map/psum | solution.py:107
  614.2 0.6 broadcast_multiply_fusion.2
  614.8 22.9 %all-reduce.3.cloned.1.call-done = f32[1024,128]{0,1:T(8,128)} async-done(((f32[1024,128]{0,1:T(8,128)}), f32[1024,128]{0,1:T(8,128)}) %all-reduce.3.cloned.1.call-update) | async-done | bytes 524304 | tf_op jit(solution)/shard_map/psum | solution.py:107
  637.7 1.1 broadcast_multiply_fusion.1
  638.8 1.0 copy.88
  639.7 372.7 %reduce-scatter.4.cloned.1.call-done = f32[64,1024]{1,0:T(8,128)} async-done(((f32[4096,1024]{1,0:T(8,128)}), f32[64,1024]{1,0:T(8,128)}) %reduce-scatter.4.cloned.1.call-update) | async-done | bytes 262160
  1012.5 1.1 copy.91
  1013.7 0.9 copy.89
  (29 shorter events, 1.5 us)
Async XLA Ops:
  7.2 38.3 %all-gather.6.cloned.1.call-start = ((), (), s32[]{:S(2)}) async-start(), calls=%async_computation.3 | async-start | bytes 2621440 | tf_op jit(solution)/shard_map/all_gather | solution.py:80
  7.9 150.1 %all-gather.4.cloned.1.call-start = ((), (), s32[]{:S(2)}) async-start(), calls=%async_computation.1 | async-start | bytes 12582912 | tf_op jit(solution)/shard_map/all_gather | solution.py:84
  8.6 629.0 %all-reduce.3.cloned.1.call-start = ((), (), s32[]{:S(2)}) async-start(), calls=%async_computation.2 | async-start | bytes 1048576 | tf_op jit(solution)/shard_map/psum | solution.py:107
  29.0 129.0 %copy-start = (bf16[1,256,1024]{2,1,0:T(8,128)(2,1)S(1)}, bf16[1,256,1024]{2,1,0:T(8,128)(2,1)}, u32[]{:S(2)}) copy-start(bf16[1,256,1024]{2,1,0:T(8,128)(2,1)} %param.9) | copy-start | bytes 1572868
  29.0 129.0 %copy-start.1 = (bf16[1,256,1024]{2,1,0:T(8,128)(2,1)S(1)}, bf16[1,256,1024]{2,1,0:T(8,128)(2,1)}, u32[]{:S(2)}) copy-start(bf16[1,256,1024]{2,1,0:T(8,128)(2,1)} %param.8) | copy-start | bytes 1572868
  29.0 129.0 %copy-start.3 = (bf16[1,256,1024]{2,1,0:T(8,128)(2,1)S(1)}, bf16[1,256,1024]{2,1,0:T(8,128)(2,1)}, u32[]{:S(2)}) copy-start(bf16[1,256,1024]{2,1,0:T(8,128)(2,1)} %param.7) | copy-start | bytes 1572868
  166.2 43.8 %collective-permute-start.1 = (bf16[127,1024]{1,0:T(8,128)(2,1)}, bf16[127,1024]{1,0:T(8,128)(2,1)}, u32[]{:S(2)}, u32[]{:S(2)}) collective-permute-start(bf16[127,1024]{1,0:T(8,128)(2,1)} %slice.121), channel_id=1, source_target_pairs={{8,0},{16,8},{24,16},{32,24},{40,32},{48,40},{56,48},{64,56},{72,6... | collective-permute-start | bytes 780296 | tf_op jit(solution)/shard_map/ppermute | solution.py:13
  207.5 99.5 %collective-permute-start = (bf16[127,1024]{1,0:T(8,128)(2,1)}, bf16[127,1024]{1,0:T(8,128)(2,1)S(1)}, u32[]{:S(2)}, u32[]{:S(2)}) collective-permute-start(bf16[127,1024]{1,0:T(8,128)(2,1)} %slice.106), channel_id=1, source_target_pairs={{0,8},{8,16},{16,24},{24,32},{32,40},{40,48},{48,56},{56,64},{64,7... | collective-permute-start | bytes 780296 | tf_op jit(solution)/shard_map/ppermute | solution.py:13
  449.6 10.6 %copy-start.4 = (f32[1024]{0:T(1024)S(1)}, f32[1024]{0:T(1024)}, u32[]{:S(2)}) copy-start(f32[1024]{0:T(1024)} %param.11) | copy-start | bytes 12292
  459.9 552.6 %reduce-scatter.4.cloned.1.call-start = ((), (), s32[]{:S(2)}) async-start(), calls=%async_computation.4 | async-start | bytes 17039360
  460.2 3.5 copy-start.2
Sparse Core Ops, SparseCore 0:
  9.8 35.6 all-gather.5
  47.3 110.6 all-gather.3
  460.0 177.6 all-reduce.2
  640.1 372.3 reduce-scatter.3
where the time goes:
time: 1030 us; the launch traced here: 1020 us
  waiting for transfers between devices  513 us (50%)
  local copies, waits for them, and re-layouts  298 us (29%)
  blocking collectives  125 us (12%)
  matrix products  48 us (5%)
  other arithmetic  17.2 us (2%)
  between operations  14.2 us (1%)
    unnamed x5, waiting for transfers between devices  374 us
    psum x1, blocking collectives, per_device(): lax.psum((lag_sums(blocks, tap_count), skip_term), ('seq', 'dp'))  125 us
    all_gather x1, waiting for transfers between devices, per_device(): lax.all_gather(out_weight, 'dp', axis=1, tiled=True)  113 us
    reshape x17, local copies, waits for them, and re-layouts, windows(): extended[lower:lower + length]  90.5 us
    concatenate x2, local copies, waits for them, and re-layouts, windows(): return jnp.concatenate(pieces, axis=1)  71.9 us
    unnamed x16, local copies, waits for them, and re-layouts  45.8 us
    psum x1, waiting for transfers between devices, per_device(): lax.psum((lag_sums(blocks, tap_count), skip_term), ('seq', 'dp'))  22.9 us
  transfers between devices with their start and end apart: 6, of which 4 were waited for; matrix products, arithmetic and copies ran while one was open for 20% of the time, Pallas kernels for 0%

commit v1 on v0

--- a/solution.py
+++ b/solution.py
@@ -104,7 +104,7 @@
         "iac,ibc->cab", signal_blocks, forward_windows, preferred_element_type=jnp.float32
     )
     skip_term = jnp.sum(signal.astype(jnp.float32) * mixed.astype(jnp.float32), axis=0)
-    filter_sum, skip_sum = lax.psum((lag_sums(blocks, tap_count), skip_term), ("seq", "dp"))
+    filter_sum, skip_sum = lax.psum(lax.psum((lag_sums(blocks, tap_count), skip_term), "dp"), "seq")
     selected = full_cot
     grad_weight = lax.psum_scatter(
         lax.dot_general(

time: 1030 us -> 1070 us (1.039)
  waiting for transfers between devices: 513 us -> 628 us
  blocking collectives: 125 us -> 53.5 us
    psum x1 -> x2, waiting for transfers between devices: 22.9 us -> 134 us  [the longest x1 134 us: per_device(): lax.psum(lax.psum((lag_sums(blocks, tap_count), skip_term), 'dp'), 'seq')]
    psum x1 -> x2, blocking collectives: 125 us -> 53.5 us  [the longest x1 47 us: per_device(): lax.psum(lax.psum((lag_sums(blocks, tap_count), skip_term), 'dp'), 'seq')]
    unnamed x5 -> x6, waiting for transfers between devices: 374 us -> 378 us
  transfers between devices with their start and end apart: 6 -> 7, of which waited for: 4 -> 4; matrix products, arithmetic and copies ran while one was open for 20% -> 20% of each run, Pallas kernels for 0% -> 0%
where the time goes in v1:
time: 1070 us; the launch traced here: 1060 us
  waiting for transfers between devices  628 us (59%)
  local copies, waits for them, and re-layouts  296 us (28%)
  blocking collectives  53.5 us (5%)
  matrix products  49.1 us (5%)
  other arithmetic  16.7 us (2%)
  between operations  14.2 us (1%)
    unnamed x6, waiting for transfers between devices  378 us
    psum x1, waiting for transfers between devices, per_device(): lax.psum(lax.psum((lag_sums(blocks, tap_count), skip_term), 'dp'), 'seq')  134 us
    all_gather x1, waiting for transfers between devices, per_device(): lax.all_gather(out_weight, 'dp', axis=1, tiled=True)  113 us
    reshape x17, local copies, waits for them, and re-layouts, windows(): extended[lower:lower + length]  90.1 us
    concatenate x2, local copies, waits for them, and re-layouts, windows(): return jnp.concatenate(pieces, axis=1)  72.2 us
    psum x1, blocking collectives, per_device(): lax.psum(lax.psum((lag_sums(blocks, tap_count), skip_term), 'dp'), 'seq')  47 us
    unnamed x16, local copies, waits for them, and re-layouts  45.7 us
  transfers between devices with their start and end apart: 7, of which 4 were waited for; matrix products, arithmetic and copies ran while one was open for 20% of the time, Pallas kernels for 0%

profile of v1, /device:TPU:64, one launch (start us, length us, event | category | flops | bytes accessed | tf_op | source)
XLA Modules:
  0.0 1063.1 jit_solution(748462047921029681)
XLA Ops:
  7.2 0.7 all-gather.6.cloned.1.call-update
  7.9 0.7 all-gather.4.cloned.1.call-update
  8.8 3.5 rev.6
  12.3 1.2 maximum_maximum_fusion
  13.7 0.7 tile.20
  14.4 2.8 slice.134
  17.2 4.8 reshape.123
  22.0 7.0 slice.135
  29.0 12.7 %copy.93 = bf16[1024,16,144]{2,1,0:T(8,128)(2,1)} copy(bf16[1024,16,144]{0,2,1:T(8,128)(2,1)} %slice.135) | data formatting | bytes 9437184
  41.7 3.8 all-gather.6.cloned.1.call-done
  45.5 112.5 %all-gather.4.cloned.1.call-done = bf16[1024,4096]{1,0:T(8,128)(2,1)} async-done(((bf16[1024,2048]{1,0:T(8,128)(2,1)}), bf16[1024,4096]{1,0:T(8,128)(2,1)}) %all-gather.4.cloned.1.call-update) | async-done | bytes 8388624 | tf_op jit(solution)/shard_map/all_gather | solution.py:84
  158.0 7.5 fusion.8
  165.6 0.7 slice.121
  166.3 2.4 collective-permute-start.1
  168.9 4.7 copy.70
  174.2 0.7 tile.8
  174.9 2.9 slice.119
  177.8 4.8 reshape.112
  182.5 6.8 slice.120
  189.3 12.5 %copy.92 = bf16[1024,16,144]{2,1,0:T(8,128)(2,1)} copy(bf16[1024,16,144]{0,2,1:T(8,128)(2,1)} %slice.120) | data formatting | bytes 9437184
  201.8 4.7 copy.74
  206.6 2.4 collective-permute-start
  209.1 3.2 pad_maximum_fusion
  212.3 5.7 copy.75
  218.0 5.7 copy.76
  223.7 5.7 copy.77
  229.5 5.7 copy.78
  235.2 5.7 copy.79
  240.9 4.7 copy.80
  245.6 4.7 copy.81
  250.3 4.7 copy.82
  255.0 1.6 pad_maximum_fusion.3
  256.6 5.7 copy.62
  262.3 5.8 copy.63
  268.1 5.7 copy.64
  273.8 5.7 copy.65
  279.5 5.7 copy.66
  285.2 4.7 copy.67
  289.9 4.7 copy.68
  294.7 4.7 copy.69
  299.3 36.1 %concatenate.41 = bf16[16,144,1024]{1,0,2:T(8,128)(2,1)} concatenate(bf16[16,16,1024]{1,0,2:T(8,128)(2,1)} %copy.62, bf16[16,16,1024]{1,0,2:T(8,128)(2,1)} %copy.63, bf16[16,16,1024]{1,0,2:T(8,128)(2,1)} %copy.64, bf16[16,16,1024]{1,0,2:T(8,128)(2,1)} %copy.65, bf16[16,16,1024]{1,0,2:T(8,128)(2,1)} %copy.66, bf16[16,16,1024]{1,0,2:T(8,128)(2,1)} %copy.67, ...), dimensions={1} | concatenate | bytes 9437184 | tf_op jit(solution)/shard_map/concatenate | solution.py:47
  335.5 11.4 %convolution_bitcast_fusion.2 = f32[16,16,1024]{1,0,2:T(8,128)} fusion(bf16[16,144,1024]{1,0,2:T(8,128)(2,1)} %concatenate.41, bf16[1024,16,144]{2,1,0:T(8,128)(2,1)} %copy.92), kind=kOutput, calls=%fused_computation.3 | convolution fusion | flops 75497472 | bytes 10485760 | tf_op jit(solution)/shard_map/cab,ibc->iac/dot_general | solution.py:72
  346.8 9.3 fusion.29
  356.1 15.0 %copy.87 = f32[1024,16,144]{0,2,1:T(8,128)} copy(f32[1024,16,144]{2,1,0:T(8,128)} %fusion.29) | data formatting | bytes 18874368 | tf_op jit(solution)/shard_map/iac,ibc->cab/dot_general | solution.py:103
  371.1 9.2 concatenate.47
  380.2 10.4 reshape.126
  390.7 4.7 slice_reduce_fusion
  395.4 2.6 rev.7
  398.1 36.1 %concatenate.45 = bf16[16,144,1024]{1,0,2:T(8,128)(2,1)} concatenate(bf16[16,16,1024]{1,0,2:T(8,128)(2,1)} %copy.74, bf16[16,16,1024]{1,0,2:T(8,128)(2,1)} %copy.75, bf16[16,16,1024]{1,0,2:T(8,128)(2,1)} %copy.76, bf16[16,16,1024]{1,0,2:T(8,128)(2,1)} %copy.77, bf16[16,16,1024]{1,0,2:T(8,128)(2,1)} %copy.78, bf16[16,16,1024]{1,0,2:T(8,128)(2,1)} %copy.79, ...), dimensions={1} | concatenate | bytes 9437184 | tf_op jit(solution)/shard_map/concatenate | solution.py:47
  434.1 11.2 %convolution_bitcast_fusion.1 = f32[16,16,1024]{1,0,2:T(8,128)} fusion(bf16[16,144,1024]{1,0,2:T(8,128)(2,1)} %concatenate.45, bf16[1024,16,144]{2,1,0:T(8,128)(2,1)} %copy.93), kind=kOutput, calls=%fused_computation.2 | convolution fusion | flops 75497472 | bytes 10485760 | tf_op jit(solution)/shard_map/cab,ibc->iac/dot_general | solution.py:93
  445.4 5.1 copy.85
  450.5 6.0 copy.73
  456.5 3.7 fusion.14
  460.5 9.7 convolution_bitcast_fusion
  470.3 17.5 %copy.90 = f32[4096,1024]{1,0:T(8,128)} copy(f32[4096,1024]{0,1:T(8,128)} %convolution_bitcast_fusion) | data formatting | bytes 33554432
  487.8 6.5 psum.30
  494.2 47.0 %psum.31 = f32[1024]{0:T(1024)S(1)} all-reduce(f32[1024]{0:T(1024)S(1)} %psum.30), channel_id=1, replica_groups=mesh['seq'=32,'tp'=4,'dp'=2] {'seq'}, use_global_device_ids=true, to_apply=%region_5.0 | all-reduce | flops 1024 | bytes 8192 | tf_op jit(solution)/shard_map/psum | solution.py:107
  541.2 0.6 broadcast_multiply_fusion.2
  541.8 134.2 %all-reduce.6.cloned.1.call-done = f32[1024,128]{0,1:T(8,128)} async-done(((f32[1024,128]{0,1:T(8,128)}), f32[1024,128]{0,1:T(8,128)}) %all-reduce.6.cloned.1.call-update) | async-done | bytes 524304 | tf_op jit(solution)/shard_map/psum | solution.py:107
  676.0 1.1 broadcast_multiply_fusion.1
  677.1 1.0 copy.88
  678.1 376.1 %reduce-scatter.4.cloned.1.call-done = f32[64,1024]{1,0:T(8,128)} async-done(((f32[4096,1024]{1,0:T(8,128)}), f32[64,1024]{1,0:T(8,128)}) %reduce-scatter.4.cloned.1.call-update) | async-done | bytes 262160
  1054.2 1.1 copy.91
  1055.4 0.9 copy.89
  (33 shorter events, 1.6 us)
Async XLA Ops:
  7.2 38.3 %all-gather.6.cloned.1.call-start = ((), (), s32[]{:S(2)}) async-start(), calls=%async_computation.4 | async-start | bytes 2621440 | tf_op jit(solution)/shard_map/all_gather | solution.py:80
  7.9 150.1 %all-gather.4.cloned.1.call-start = ((), (), s32[]{:S(2)}) async-start(), calls=%async_computation.1 | async-start | bytes 12582912 | tf_op jit(solution)/shard_map/all_gather | solution.py:84
  8.6 451.6 %all-reduce.4.cloned.1.call-start = ((), (), s32[]{:S(2)}) async-start(), calls=%async_computation.2 | async-start | bytes 1048576 | tf_op jit(solution)/shard_map/psum | solution.py:107
  29.0 129.0 %copy-start.1 = (bf16[1,256,1024]{2,1,0:T(8,128)(2,1)S(1)}, bf16[1,256,1024]{2,1,0:T(8,128)(2,1)}, u32[]{:S(2)}) copy-start(bf16[1,256,1024]{2,1,0:T(8,128)(2,1)} %param.9) | copy-start | bytes 1572868
  29.0 129.0 %copy-start.2 = (bf16[1,256,1024]{2,1,0:T(8,128)(2,1)S(1)}, bf16[1,256,1024]{2,1,0:T(8,128)(2,1)}, u32[]{:S(2)}) copy-start(bf16[1,256,1024]{2,1,0:T(8,128)(2,1)} %param.8) | copy-start | bytes 1572868
  29.0 129.0 %copy-start.3 = (bf16[1,256,1024]{2,1,0:T(8,128)(2,1)S(1)}, bf16[1,256,1024]{2,1,0:T(8,128)(2,1)}, u32[]{:S(2)}) copy-start(bf16[1,256,1024]{2,1,0:T(8,128)(2,1)} %param.7) | copy-start | bytes 1572868
  166.3 42.7 %collective-permute-start.1 = (bf16[127,1024]{1,0:T(8,128)(2,1)}, bf16[127,1024]{1,0:T(8,128)(2,1)}, u32[]{:S(2)}, u32[]{:S(2)}) collective-permute-start(bf16[127,1024]{1,0:T(8,128)(2,1)} %slice.121), channel_id=1, source_target_pairs={{8,0},{16,8},{24,16},{32,24},{40,32},{48,40},{56,48},{64,56},{72,6... | collective-permute-start | bytes 780296 | tf_op jit(solution)/shard_map/ppermute | solution.py:13
  206.6 48.4 %collective-permute-start = (bf16[127,1024]{1,0:T(8,128)(2,1)S(1)}, bf16[127,1024]{1,0:T(8,128)(2,1)S(1)}, u32[]{:S(2)}, u32[]{:S(2)}) collective-permute-start(bf16[127,1024]{1,0:T(8,128)(2,1)S(1)} %slice.106), channel_id=1, source_target_pairs={{0,8},{8,16},{16,24},{24,32},{32,40},{40,48},{48,56},{56,64},{64,7... | collective-permute-start | bytes 780296 | tf_op jit(solution)/shard_map/ppermute | solution.py:13
  335.5 11.4 %copy-start = (bf16[16,16,1024]{1,0,2:T(8,128)(2,1)S(1)}, bf16[16,16,1024]{1,0,2:T(8,128)(2,1)}, u32[]{:S(2)}) copy-start(bf16[16,16,1024]{1,0,2:T(8,128)(2,1)} %copy.74) | copy-start | bytes 1572868
  398.0 278.0 %all-reduce.6.cloned.1.call-start = ((), (), s32[]{:S(2)}) async-start(), calls=%async_computation.3 | async-start | bytes 1048576 | tf_op jit(solution)/shard_map/psum | solution.py:107
  445.3 11.1 %copy-start.4 = (f32[1024]{0:T(1024)S(1)}, f32[1024]{0:T(1024)}, u32[]{:S(2)}) copy-start(f32[1024]{0:T(1024)} %param.11) | copy-start | bytes 12292
  460.2 594.0 %reduce-scatter.4.cloned.1.call-start = ((), (), s32[]{:S(2)}) async-start(), calls=%async_computation.5 | async-start | bytes 17039360
Sparse Core Ops, SparseCore 0:
  9.8 35.6 all-gather.5
  47.3 110.6 all-gather.3
  398.2 41.9 all-reduce.3
  460.4 215.6 all-reduce.5
  678.4 375.7 reduce-scatter.3
